TPU v7x, 32 devices: a whole 2x2x4 slice. The times are simulated.
32 devices in a mesh: dp: 8 (over z, y), tensor: 4 (over x, core).
Axes of the slice: x: 2, y: 2, z: 4, core: 2. Of those that a mesh axis runs over, the one named last changes fastest.
Arguments:
- inputs: bfloat16 [608, 8, 1024], P('tensor', 'dp'), may hold values from -6 to 6
- attn_gain: bfloat16 [2, 1024], P(None, 'dp'), may hold values from 0.5 to 1.5
- attn_shift: bfloat16 [2, 1024], P(None, 'dp'), may hold values from -1.25 to 1.25
- qkv_weight: bfloat16 [2, 1024, 3, 1024], P(None, 'dp', None, 'tensor'), may hold values from -0.1875 to 0.1875
- query_bias: bfloat16 [2, 1024], P(None, 'dp'), may hold values from -3 to 3
- value_bias: bfloat16 [2, 1024], P(None, 'dp'), may hold values from -1.25 to 1.25
- out_weight: bfloat16 [2, 1024, 1024], P(None, 'tensor', 'dp'), may hold values from -2 to 2
- out_bias: bfloat16 [2, 1024], P(None, 'dp'), may hold values from -1.25 to 1.25
- mlp_gain: bfloat16 [2, 1024], P(None, 'dp'), may hold values from 0.5 to 1.5
- mlp_shift: bfloat16 [2, 1024], P(None, 'dp'), may hold values from -1.25 to 1.25
- up_weight: bfloat16 [2, 1024, 4096], P(None, 'dp', 'tensor'), may hold values from -0.1875 to 0.1875
- up_bias: bfloat16 [2, 4096], P(None, 'dp'), may hold values from -1.25 to 1.25
- down_weight: bfloat16 [2, 4096, 1024], P(None, 'tensor', 'dp'), may hold values from -0.09375 to 0.09375
- down_bias: bfloat16 [2, 1024], P(None, 'dp'), may hold values from -1.25 to 1.25
- cotangent: bfloat16 [608, 8, 1024], P('tensor', 'dp'), may hold values from -6 to 6
- image_mask: int32 [8], P('dp'), may hold values 0 or 1
- row_mask: int32 [608, 8], P(None, 'dp'), may hold values from 0 to 1, as said below
Outputs:
- outputs: bfloat16 [608, 8, 1024], P('tensor', 'dp')
- grad_inputs: float32 [608, 8, 1024], P('tensor', 'dp')
- grad_attn_gain: float32 [2, 1024], P(None, 'dp')
- grad_attn_shift: float32 [2, 1024], P(None, 'dp')
- grad_qkv_weight: float32 [2, 1024, 3, 1024], P(None, 'dp', None, 'tensor')
- grad_query_bias: float32 [2, 1024], P(None, 'dp')
- grad_value_bias: float32 [2, 1024], P(None, 'dp')
- grad_out_weight: float32 [2, 1024, 1024], P(None, 'tensor', 'dp')
- grad_out_bias: float32 [2, 1024], P(None, 'dp')
- grad_mlp_gain: float32 [2, 1024], P(None, 'dp')
- grad_mlp_shift: float32 [2, 1024], P(None, 'dp')
- grad_up_weight: float32 [2, 1024, 4096], P(None, 'dp', 'tensor')
- grad_up_bias: float32 [2, 4096], P(None, 'dp')
- grad_down_weight: float32 [2, 4096, 1024], P(None, 'tensor', 'dp')
- grad_down_bias: float32 [2, 1024], P(None, 'dp')
Inputs may be any that keep to these rules, and one draw needn't show every extreme that they name: `row_mask`: row 0 of every image is live; rows 577 and later are 0.
All inputs are finite; a program needn't handle non-finite values. No bound on the sum of `image_mask` on one device may be relied on, other than what follows from the above.
Results may differ from a plain program's by a relative error of at most 0.015.
Values may be sent and summed in bfloat16 or wider, within the bound.
A program may use at most 128 MiB of HBM per device.

v0:
```python
import jax
import jax.numpy as jnp
from jax import lax
from jax.sharding import PartitionSpec as P

HEAD_DIM = 64


def layer_norm(values, gain, shift):
    center = values - jnp.mean(values, -1, keepdims=True)
    inverse = lax.rsqrt(jnp.mean(center * center, -1, keepdims=True) + 1e-05)
    return center * inverse * gain + shift


def norm_backward(values, gain, grad_out):
    center = values - jnp.mean(values, -1, keepdims=True)
    inverse = lax.rsqrt(jnp.mean(center * center, -1, keepdims=True) + 1e-05)
    normal = center * inverse
    grad_hat = grad_out * gain
    grad_in = inverse * (
        grad_hat
        - jnp.mean(grad_hat, -1, keepdims=True)
        - normal * jnp.mean(grad_hat * normal, -1, keepdims=True)
    )
    return (grad_in, jnp.sum(grad_out * normal, (0, 1)), jnp.sum(grad_out, (0, 1)))


def quick_gelu(values):
    return values * jax.nn.sigmoid(1.702 * values)


def gelu_slope(values):
    sigma = jax.nn.sigmoid(1.702 * values)
    return sigma + 1.702 * values * sigma * (1.0 - sigma)


def image_scores(block, keep):
    scores = jnp.einsum(
        "qhe,khe->hqk", block[:, 0], block[:, 1], preferred_element_type=jnp.float32
    )
    scores = scores * HEAD_DIM ** (-0.5)
    return jnp.where(keep[None, None, :], scores, -1e30)


def attention_forward(qkv, row_mask):
    seq_len, images, width = (qkv.shape[0], qkv.shape[1], qkv.shape[3])
    heads = width // HEAD_DIM

    def one_image(which, carry):
        outs, lses = carry
        block = lax.dynamic_index_in_dim(qkv, which, 1, keepdims=False).reshape(
            seq_len, 3, heads, HEAD_DIM
        )
        keep = lax.dynamic_index_in_dim(row_mask, which, 1, keepdims=False) > 0
        scores = image_scores(block, keep)
        row_max = jnp.max(scores, -1, keepdims=True)
        expo = jnp.exp(scores - row_max)
        row_total = jnp.sum(expo, -1, keepdims=True)
        weights = (expo / row_total).astype(jnp.bfloat16)
        values = jnp.einsum(
            "hqk,khe->qhe", weights, block[:, 2], preferred_element_type=jnp.float32
        )
        values = values.astype(jnp.bfloat16).reshape(seq_len, 1, width)
        outs = values
        lses = lax.dynamic_update_index_in_dim(
            lses, (row_max + jnp.log(row_total))[:, :, 0], which, 0
        )
        return (outs, lses)

    start = (
        jnp.zeros((seq_len, images, width), jnp.bfloat16),
        jnp.zeros((images, heads, seq_len), jnp.float32),
    )
    return lax.fori_loop(0, images, one_image, start)


def attention_backward(qkv, lses, grad_mixed, row_mask):
    seq_len, images, width = (qkv.shape[0], qkv.shape[1], qkv.shape[3])
    heads = width // HEAD_DIM
    scale = HEAD_DIM ** (-0.5)

    def one_image(which, grads):
        block = lax.dynamic_index_in_dim(qkv, which, 1, keepdims=False).reshape(
            seq_len, 3, heads, HEAD_DIM
        )
        keep = lax.dynamic_index_in_dim(row_mask, which, 1, keepdims=False) > 0
        grad_out = lax.dynamic_index_in_dim(grad_mixed, which, 1, keepdims=False).reshape(
            seq_len, heads, HEAD_DIM
        )
        lse_here = lax.dynamic_index_in_dim(lses, which, 0, keepdims=False)
        weights = jnp.exp(image_scores(block, keep) - lse_here[:, :, None])
        grad_value = jnp.einsum(
            "hqk,qhe->khe",
            weights.astype(jnp.bfloat16),
            grad_out,
            preferred_element_type=jnp.float32,
        )
        grad_weights = jnp.einsum(
            "qhe,khe->hqk", grad_out, block[:, 2], preferred_element_type=jnp.float32
        )
        delta = jnp.sum(weights * grad_weights, -1, keepdims=True)
        grad_scores = (weights * (grad_weights - delta)).astype(jnp.bfloat16)
        grad_query = (
            jnp.einsum("hqk,khe->qhe", grad_scores, block[:, 1], preferred_element_type=jnp.float32)
            * scale
        )
        grad_key = (
            jnp.einsum("hqk,qhe->khe", grad_scores, block[:, 0], preferred_element_type=jnp.float32)
            * scale
        )
        stacked = jnp.stack([grad_query, grad_key, grad_value], 1).astype(jnp.bfloat16)
        return stacked.reshape(seq_len, 1, 3, width)

    return lax.fori_loop(0, images, one_image, jnp.zeros(qkv.shape, jnp.bfloat16))


def body(
    inputs,
    attn_gain,
    attn_shift,
    qkv_weight,
    query_bias,
    value_bias,
    out_weight,
    out_bias,
    mlp_gain,
    mlp_shift,
    up_weight,
    up_bias,
    down_weight,
    down_bias,
    cotangent,
    image_mask,
    row_mask,
):
    depth_count = qkv_weight.shape[0]
    tensor_rank = lax.axis_index("tensor")
    local_rows = inputs.shape[0]
    head_width = qkv_weight.shape[3]
    unit_width = up_weight.shape[2]
    vectors = jnp.stack(
        [attn_gain, attn_shift, query_bias, value_bias, out_bias, mlp_gain, mlp_shift, down_bias], 1
    )

    def fetch(depth):
        return (
            lax.all_gather(qkv_weight[depth], "dp", axis=0, tiled=True),
            lax.all_gather(up_weight[depth], "dp", axis=0, tiled=True),
            lax.all_gather(out_weight[depth], "dp", axis=1, tiled=True),
            lax.all_gather(down_weight[depth], "dp", axis=1, tiled=True),
            lax.all_gather(vectors[depth], "dp", axis=1, tiled=True),
            lax.all_gather(up_bias[depth], "dp", axis=0, tiled=True),
        )

    def unpack(weights):
        vec = weights[4].astype(jnp.float32)
        query_cols = lax.dynamic_slice_in_dim(vec[2], tensor_rank * head_width, head_width)
        value_cols = lax.dynamic_slice_in_dim(vec[3], tensor_rank * head_width, head_width)
        bias_three = jnp.stack([query_cols, jnp.zeros_like(query_cols), value_cols])
        up_cols = lax.dynamic_slice_in_dim(
            weights[5].astype(jnp.float32), tensor_rank * unit_width, unit_width
        )
        return (vec, bias_three, up_cols)

    def forward_parts(hidden, weights):
        qkv_w, up_w, out_w = (weights[0], weights[1], weights[2])
        vec, bias_three, up_cols = unpack(weights)
        normed = layer_norm(hidden, vec[0], vec[1]).astype(jnp.bfloat16)
        product = jnp.einsum(
            "sid,dce->sice",
            lax.all_gather(normed, "tensor", axis=0, tiled=True),
            qkv_w,
            preferred_element_type=jnp.float32,
        )
        qkv = (product + bias_three).astype(jnp.bfloat16)
        mixed, lses = attention_forward(qkv, row_mask)
        middle = (
            hidden
            + lax.psum_scatter(
                jnp.einsum("sie,ed->sid", mixed, out_w, preferred_element_type=jnp.float32).astype(
                    jnp.bfloat16
                ),
                "tensor",
                scatter_dimension=0,
                tiled=True,
            ).astype(jnp.float32)
            + vec[4]
        )
        normed_mid = layer_norm(middle, vec[5], vec[6]).astype(jnp.bfloat16)
        before = (
            jnp.einsum(
                "sid,df->sif",
                lax.all_gather(normed_mid, "tensor", axis=0, tiled=True),
                up_w,
                preferred_element_type=jnp.float32,
            )
            + up_cols
        )
        active = quick_gelu(before).astype(jnp.bfloat16)
        return (normed, qkv, mixed, lses, middle, normed_mid, before, active)

    hidden = inputs.astype(jnp.float32)
    kept = []
    layer_inputs = []
    stored = []
    for depth in range(depth_count):
        weights = fetch(depth)
        kept.append(weights)
        layer_inputs.append(hidden)
        parts = forward_parts(hidden, weights)
        stored.append(parts)
        down_cols = weights[4][7].astype(jnp.float32)
        mlp_active = parts[7]
        mlp_down_w = weights[3]
        hidden = (
            parts[4]
            + lax.psum_scatter(
                jnp.einsum(
                    "sif,fd->sid", mlp_active, mlp_down_w, preferred_element_type=jnp.float32
                ).astype(jnp.bfloat16),
                "tensor",
                scatter_dimension=0,
                tiled=True,
            ).astype(jnp.float32)
            + down_cols
        )
    live_rows = lax.dynamic_slice_in_dim(row_mask, tensor_rank * local_rows, local_rows, 0)
    live = (live_rows * image_mask[None, :]).astype(jnp.float32)
    grad = cotangent.astype(jnp.float32) * live[:, :, None]
    per_layer = []
    for depth in reversed(range(depth_count)):
        weights = fetch(depth)
        parts = forward_parts(layer_inputs[depth], weights)
        layer_qkv_w = weights[0]
        layer_up_w = weights[1]
        layer_out_w = weights[2]
        down_w = weights[3]
        layer_vec, layer_bias_three, layer_up_cols = unpack(weights)
        (
            layer_normed,
            layer_qkv,
            layer_mixed,
            layer_lses,
            layer_middle,
            layer_normed_mid,
            layer_before,
            layer_active,
        ) = parts
        full_width = layer_vec.shape[1]
        grad_down_bias = jnp.sum(grad, (0, 1))
        fold_piece = lax.all_gather(grad.astype(jnp.bfloat16), "tensor", axis=0, tiled=True)
        update = jnp.einsum("sid,fd->sif", fold_piece, down_w, preferred_element_type=jnp.float32)
        grad_down_w = jnp.einsum(
            "sif,sid->fd", layer_active, fold_piece, preferred_element_type=jnp.float32
        )
        grad_before = (update * gelu_slope(layer_before)).astype(jnp.bfloat16)
        grad_up_cols = jnp.sum(grad_before.astype(jnp.float32), (0, 1))
        grad_up_w = jnp.einsum(
            "sid,sif->df",
            lax.all_gather(layer_normed_mid, "tensor", axis=0, tiled=True),
            grad_before,
            preferred_element_type=jnp.float32,
        )
        grad_normed_mid = lax.psum_scatter(
            jnp.einsum(
                "sif,df->sid", grad_before, layer_up_w, preferred_element_type=jnp.float32
            ).astype(jnp.bfloat16),
            "tensor",
            scatter_dimension=0,
            tiled=True,
        ).astype(jnp.float32)
        grad_mid, grad_mlp_gain, grad_mlp_shift = norm_backward(
            layer_middle, layer_vec[5], grad_normed_mid
        )
        grad_mid = grad_mid + grad
        grad_out_bias = jnp.sum(grad_mid, (0, 1))
        piece = lax.all_gather(grad_mid.astype(jnp.bfloat16), "tensor", axis=0, tiled=True)
        fold_update = jnp.einsum(
            "sid,ed->sie", piece, layer_out_w, preferred_element_type=jnp.float32
        )
        grad_out_w = jnp.einsum(
            "sie,sid->ed", layer_mixed, piece, preferred_element_type=jnp.float32
        )
        grad_qkv = attention_backward(
            layer_qkv, layer_lses, fold_update.astype(jnp.bfloat16), row_mask
        )
        grad_bias_three = jnp.sum(grad_qkv.astype(jnp.float32), (0, 1))
        grad_qkv_w = jnp.einsum(
            "sid,sice->dce",
            lax.all_gather(layer_normed, "tensor", axis=0, tiled=True),
            grad_qkv,
            preferred_element_type=jnp.float32,
        )
        grad_normed = lax.psum_scatter(
            jnp.einsum(
                "sice,dce->sid", grad_qkv, layer_qkv_w, preferred_element_type=jnp.float32
            ).astype(jnp.bfloat16),
            "tensor",
            scatter_dimension=0,
            tiled=True,
        ).astype(jnp.float32)
        grad_in, grad_attn_gain, grad_attn_shift = norm_backward(
            layer_inputs[depth], layer_vec[0], grad_normed
        )
        grad_in = grad_in + grad_mid
        empty = jnp.zeros((full_width,), jnp.float32)
        grad_query = lax.dynamic_update_slice_in_dim(
            empty, grad_bias_three[0], tensor_rank * head_width, 0
        )
        grad_value = lax.dynamic_update_slice_in_dim(
            empty, grad_bias_three[2], tensor_rank * head_width, 0
        )
        grad_up_full = lax.dynamic_update_slice_in_dim(
            jnp.zeros((weights[5].shape[0],), jnp.float32),
            grad_up_cols,
            tensor_rank * unit_width,
            0,
        )
        grad_vec = jnp.stack(
            [
                grad_attn_gain,
                grad_attn_shift,
                grad_query,
                grad_value,
                grad_out_bias,
                grad_mlp_gain,
                grad_mlp_shift,
                grad_down_bias,
            ]
        )
        shards = (
            lax.psum_scatter(grad_qkv_w, "dp", scatter_dimension=0, tiled=True),
            lax.psum_scatter(grad_up_w, "dp", scatter_dimension=0, tiled=True),
            lax.psum_scatter(grad_out_w, "dp", scatter_dimension=1, tiled=True),
            lax.psum_scatter(grad_down_w, "dp", scatter_dimension=1, tiled=True),
            lax.psum_scatter(grad_vec, "dp", scatter_dimension=1, tiled=True),
            lax.psum_scatter(grad_up_full, "dp", scatter_dimension=0, tiled=True),
        )
        grad, shards = (grad_in, shards)
        per_layer.insert(0, shards)
    vec_grads = jnp.stack([shards[4] for shards in per_layer])
    bias_grads = jnp.stack([shards[5] for shards in per_layer])
    vec_sum, up_sum = lax.psum((vec_grads, bias_grads), "tensor")
    return (
        hidden.astype(jnp.bfloat16),
        grad,
        vec_sum[:, 0],
        vec_sum[:, 1],
        jnp.stack([shards[0] for shards in per_layer]),
        vec_sum[:, 2],
        vec_sum[:, 3],
        jnp.stack([shards[2] for shards in per_layer]),
        vec_sum[:, 4],
        vec_sum[:, 5],
        vec_sum[:, 6],
        jnp.stack([shards[1] for shards in per_layer]),
        up_sum,
        jnp.stack([shards[3] for shards in per_layer]),
        vec_sum[:, 7],
    )


def solution(mesh):
    in_specs = (
        P("tensor", "dp", None),
        P(None, "dp"),
        P(None, "dp"),
        P(None, "dp", None, "tensor"),
        P(None, "dp"),
        P(None, "dp"),
        P(None, "tensor", "dp"),
        P(None, "dp"),
        P(None, "dp"),
        P(None, "dp"),
        P(None, "dp", "tensor"),
        P(None, "dp"),
        P(None, "tensor", "dp"),
        P(None, "dp"),
        P("tensor", "dp", None),
        P("dp"),
        P(None, "dp"),
    )
    out_specs = (
        P("tensor", "dp", None),
        P("tensor", "dp", None),
        P(None, "dp"),
        P(None, "dp"),
        P(None, "dp", None, "tensor"),
        P(None, "dp"),
        P(None, "dp"),
        P(None, "tensor", "dp"),
        P(None, "dp"),
        P(None, "dp"),
        P(None, "dp"),
        P(None, "dp", "tensor"),
        P(None, "dp"),
        P(None, "tensor", "dp"),
        P(None, "dp"),
    )
    return jax.shard_map(body, mesh=mesh, in_specs=in_specs, out_specs=out_specs, check_vma=False)
```

profile of v0, /device:TPU:0, one launch (start us, length us, event | category | flops | bytes accessed | tf_op | source)
XLA Modules:
  0.0 1578.2 jit_solution(11736033393084943452)
XLA Ops:
  14.9 22.4 %all-gather = bf16[1,8,1024]{2,0,1:T(2,128)(2,1)S(1)} all-gather(bf16[1,8,128]{2,0,1:T(2,128)(2,1)S(1)} %get-tuple-element.224), channel_id=2, replica_groups=mesh['dp'=8,'tensor'=4] {'dp'}, dimensions={2}, use_global_device_ids=true | all-gather | bytes 18432 | tf_op jit(solution)/shard_map/all_gather | solution.py:151
  58.0 28.1 %all-gather.2 = bf16[1,256,1024]{2,1,0:T(8,128)(2,1)S(1)} all-gather(bf16[1,256,128]{2,1,0:T(8,128)(2,1)S(1)} %get-tuple-element.201), channel_id=4, replica_groups=mesh['dp'=8,'tensor'=4] {'dp'}, dimensions={2}, use_global_device_ids=true | all-gather | bytes 589824 | tf_op jit(solution)/shard_map/all_gather | solution.py:149
  115.2 24.1 %reduce-scatter.19.cloned.1.call-done = bf16[152,1,1024]{2,0,1:T(8,128)(2,1)} async-done(((bf16[608,1,1024]{2,0,1:T(8,128)(2,1)}), bf16[152,1,1024]{2,0,1:T(8,128)(2,1)}) %reduce-scatter.19.cloned.1.call-update) | async-done | bytes 311312 | tf_op jit(solution)/shard_map/reduce_scatter | solution.py:179
  144.7 26.2 %all-gather.4 = bf16[1,4096]{1,0:T(2,128)(2,1)S(1)} all-gather(bf16[1,512]{1,0:T(2,128)(2,1)S(1)} %get-tuple-element.227), channel_id=6, replica_groups=mesh['dp'=8,'tensor'=4] {'dp'}, dimensions={1}, use_global_device_ids=true | all-gather | bytes 9216 | tf_op jit(solution)/shard_map/all_gather | solution.py:152
  214.8 48.9 %all-gather.47.cloned.1.call-done = bf16[1,1024,1024]{2,1,0:T(8,128)(2,1)} async-done(((bf16[1,1024,128]{2,1,0:T(8,128)(2,1)}), bf16[1,1024,1024]{2,1,0:T(8,128)(2,1)}) %all-gather.47.cloned.1.call-update) | async-done | bytes 2097168 | tf_op jit(solution)/shard_map/all_gather | solution.py:150
  269.5 23.6 %reduce-scatter.21.cloned.1.call-done = bf16[152,1,1024]{2,0,1:T(8,128)(2,1)} async-done(((bf16[608,1,1024]{2,0,1:T(8,128)(2,1)}), bf16[152,1,1024]{2,0,1:T(8,128)(2,1)}) %reduce-scatter.21.cloned.1.call-update) | async-done | bytes 311312 | tf_op jit(solution)/shard_map/reduce_scatter | solution.py:217
  295.5 30.9 %all-gather.8 = bf16[1,256,1024]{2,1,0:T(8,128)(2,1)} all-gather(bf16[1,256,128]{2,1,0:T(8,128)(2,1)S(1)} %get-tuple-element.200), channel_id=10, replica_groups=mesh['dp'=8,'tensor'=4] {'dp'}, dimensions={2}, use_global_device_ids=true | all-gather | bytes 589824 | tf_op jit(solution)/shard_map/all_gather | solution.py:149
  374.6 25.5 %reduce-scatter.23.cloned.1.call-done = bf16[152,1,1024]{2,0,1:T(8,128)(2,1)} async-done(((bf16[608,1,1024]{2,0,1:T(8,128)(2,1)}), bf16[152,1,1024]{2,0,1:T(8,128)(2,1)}) %reduce-scatter.23.cloned.1.call-update) | async-done | bytes 311312 | tf_op jit(solution)/shard_map/reduce_scatter | solution.py:179
  404.7 26.2 %all-gather.10 = bf16[1,4096]{1,0:T(2,128)(2,1)S(1)} all-gather(bf16[1,512]{1,0:T(2,128)(2,1)S(1)} %get-tuple-element.226), channel_id=12, replica_groups=mesh['dp'=8,'tensor'=4] {'dp'}, dimensions={1}, use_global_device_ids=true | all-gather | bytes 9216 | tf_op jit(solution)/shard_map/all_gather | solution.py:152
  430.9 21.5 %all-gather.51.cloned.1.call-done = bf16[1,1024,1024]{2,1,0:T(8,128)(2,1)} async-done(((bf16[1,128,1024]{2,1,0:T(8,128)(2,1)}), bf16[1,1024,1024]{2,1,0:T(8,128)(2,1)}) %all-gather.51.cloned.1.call-update) | async-done | bytes 2097168 | tf_op jit(solution)/shard_map/all_gather | solution.py:148
  490.9 53.2 %all-gather.53.cloned.1.call-done = bf16[1,1024,1024]{2,1,0:T(8,128)(2,1)} async-done(((bf16[1,1024,128]{2,1,0:T(8,128)(2,1)}), bf16[1,1024,1024]{2,1,0:T(8,128)(2,1)}) %all-gather.53.cloned.1.call-update) | async-done | bytes 2097168 | tf_op jit(solution)/shard_map/all_gather | solution.py:150
  579.8 26.6 %reduce-scatter.25.cloned.1.call-done = bf16[152,1,1024]{2,0,1:T(8,128)(2,1)} async-done(((bf16[608,1,1024]{2,0,1:T(8,128)(2,1)}), bf16[152,1,1024]{2,0,1:T(8,128)(2,1)}) %reduce-scatter.25.cloned.1.call-update) | async-done | bytes 311312 | tf_op jit(solution)/shard_map/reduce_scatter | solution.py:217
  651.1 26.2 %reduce-scatter.29.cloned.1.call-done = bf16[152,1,1024]{2,0,1:T(8,128)(2,1)} async-done(((bf16[608,1,1024]{2,0,1:T(8,128)(2,1)}), bf16[152,1,1024]{2,0,1:T(8,128)(2,1)}) %reduce-scatter.29.cloned.1.call-update) | async-done | bytes 311312 | tf_op jit(solution)/shard_map/reduce_scatter | solution.py:294
  708.1 25.8 %reduce-scatter.31.cloned.1.call-done = bf16[152,1,1024]{2,0,1:T(8,128)(2,1)} async-done(((bf16[608,1,1024]{2,0,1:T(8,128)(2,1)}), bf16[152,1,1024]{2,0,1:T(8,128)(2,1)}) %reduce-scatter.31.cloned.1.call-update) | async-done | bytes 311312 | tf_op jit(solution)/shard_map/reduce_scatter | solution.py:264
  840.4 37.1 %all-reduce.2 = (f32[4096]{0:T(1024)S(1)}, f32[4096]{0:T(1024)S(1)}) all-reduce(f32[4096]{0:T(1024)S(1)} %dynamic_update_slice.32, f32[4096]{0:T(1024)S(1)} %dynamic_update_slice.31), channel_id=31, replica_groups=mesh['dp'=8,'tensor'=4] {'dp'}, use_global_device_ids=true, to_apply=%region_56.57.clone | all-reduce | flops 8192 | bytes 65536
  877.7 58.1 %reduce-scatter.43.cloned.1.call-done = f32[256,128]{1,0:T(8,128)} async-done(((f32[256,1024]{1,0:T(8,128)}), f32[256,128]{1,0:T(8,128)}) %reduce-scatter.43.cloned.1.call-update) | async-done | bytes 131088 | tf_op jit(solution)/shard_map/reduce_scatter | solution.py:334
  939.2 52.2 %reduce-scatter.37.cloned.1.call-done = f32[8,128]{1,0:T(8,128)} async-done(((f32[8,1024]{1,0:T(8,128)}), f32[8,128]{1,0:T(8,128)}) %reduce-scatter.37.cloned.1.call-update) | async-done | bytes 4112 | tf_op jit(solution)/shard_map/reduce_scatter | solution.py:336
  991.4 55.6 %reduce-scatter.35.cloned.1.call-done = f32[8,128]{1,0:T(8,128)} async-done(((f32[8,1024]{1,0:T(8,128)}), f32[8,128]{1,0:T(8,128)}) %reduce-scatter.35.cloned.1.call-update) | async-done | bytes 4112 | tf_op jit(solution)/shard_map/reduce_scatter | solution.py:336
  1059.0 79.0 %reduce-scatter.53.cloned.1.call-done = f32[1024,128]{1,0:T(8,128)} async-done(((f32[1024,1024]{1,0:T(8,128)}), f32[1024,128]{1,0:T(8,128)}) %reduce-scatter.53.cloned.1.call-update) | async-done | bytes 524304 | tf_op jit(solution)/shard_map/reduce_scatter | solution.py:335
  1138.0 92.3 %reduce-scatter.51.cloned.1.call-done = f32[1024,128]{1,0:T(8,128)} async-done(((f32[1024,1024]{1,0:T(8,128)}), f32[1024,128]{1,0:T(8,128)}) %reduce-scatter.51.cloned.1.call-update) | async-done | bytes 524304 | tf_op jit(solution)/shard_map/reduce_scatter | solution.py:335
  1232.6 89.2 %reduce-scatter.49.cloned.1.call-done = f32[128,1024]{1,0:T(8,128)} async-done(((f32[1024,1024]{1,0:T(8,128)}), f32[128,1024]{1,0:T(8,128)}) %reduce-scatter.49.cloned.1.call-update) | async-done | bytes 524304 | tf_op jit(solution)/shard_map/reduce_scatter | solution.py:333
  1321.8 91.8 %reduce-scatter.47.cloned.1.call-done = f32[128,1024]{1,0:T(8,128)} async-done(((f32[1024,1024]{1,0:T(8,128)}), f32[128,1024]{1,0:T(8,128)}) %reduce-scatter.47.cloned.1.call-update) | async-done | bytes 524304 | tf_op jit(solution)/shard_map/reduce_scatter | solution.py:333
  1415.9 75.9 %reduce-scatter.41.cloned.1.call-done = f32[128,3,256]{2,0,1:T(8,128)} async-done(((f32[1024,3,256]{2,0,1:T(8,128)}), f32[128,3,256]{2,0,1:T(8,128)}) %reduce-scatter.41.cloned.1.call-update) | async-done | bytes 393232 | tf_op jit(solution)/shard_map/reduce_scatter | solution.py:332
  1491.8 77.7 %reduce-scatter.39.cloned.1.call-done = f32[128,3,256]{2,0,1:T(8,128)} async-done(((f32[1024,3,256]{2,0,1:T(8,128)}), f32[128,3,256]{2,0,1:T(8,128)}) %reduce-scatter.39.cloned.1.call-update) | async-done | bytes 393232 | tf_op jit(solution)/shard_map/reduce_scatter | solution.py:332
  (409 shorter events, 443.2 us)
Async XLA Ops:
  7.2 79.0 %all-gather.27.cloned.1.call-start = ((), (), s32[]{:S(2)}) async-start(), calls=%async_computation.18 | async-start | bytes 1556480 | tf_op jit(solution)/shard_map/all_gather | solution.py:171
  41.2 98.2 %reduce-scatter.19.cloned.1.call-start = ((), (), s32[]{:S(2)}) async-start(), calls=%async_computation.19 | async-start | bytes 1556480 | tf_op jit(solution)/shard_map/reduce_scatter | solution.py:179
  114.3 77.2 %all-gather.45.cloned.1.call-start = ((), (), s32[]{:S(2)}) async-start(), calls=%async_computation.45 | async-start | bytes 2359296 | tf_op jit(solution)/shard_map/all_gather | solution.py:148
  115.2 94.7 %all-gather.29.cloned.1.call-start = ((), (), s32[]{:S(2)}) async-start(), calls=%async_computation.20 | async-start | bytes 1556480 | tf_op jit(solution)/shard_map/all_gather | solution.py:193
  143.7 120.0 %all-gather.47.cloned.1.call-start = ((), (), s32[]{:S(2)}) async-start(), calls=%async_computation.46 | async-start | bytes 2359296 | tf_op jit(solution)/shard_map/all_gather | solution.py:150
  144.6 148.5 %reduce-scatter.21.cloned.1.call-start = ((), (), s32[]{:S(2)}) async-start(), calls=%async_computation.21 | async-start | bytes 1556480 | tf_op jit(solution)/shard_map/reduce_scatter | solution.py:217
  268.6 73.3 %all-gather.49.cloned.1.call-start = ((), (), s32[]{:S(2)}) async-start(), calls=%async_computation.47 | async-start | bytes 1769472 | tf_op jit(solution)/shard_map/all_gather | solution.py:147
  269.4 91.3 %all-gather.31.cloned.1.call-start = ((), (), s32[]{:S(2)}) async-start(), calls=%async_computation.22 | async-start | bytes 1556480 | tf_op jit(solution)/shard_map/all_gather | solution.py:171
  295.5 104.6 %reduce-scatter.23.cloned.1.call-start = ((), (), s32[]{:S(2)}) async-start(), calls=%async_computation.23 | async-start | bytes 1556480 | tf_op jit(solution)/shard_map/reduce_scatter | solution.py:179
  373.9 78.6 %all-gather.51.cloned.1.call-start = ((), (), s32[]{:S(2)}) async-start(), calls=%async_computation.48 | async-start | bytes 2359296 | tf_op jit(solution)/shard_map/all_gather | solution.py:148
  374.6 96.3 %all-gather.33.cloned.1.call-start = ((), (), s32[]{:S(2)}) async-start(), calls=%async_computation.24 | async-start | bytes 1556480 | tf_op jit(solution)/shard_map/all_gather | solution.py:193
  402.4 88.5 %all-gather.35.cloned.1.call-start = ((), (), s32[]{:S(2)}) async-start(), calls=%async_computation.26 | async-start | bytes 1556480 | tf_op jit(solution)/shard_map/all_gather | solution.py:251
  404.1 140.1 %all-gather.53.cloned.1.call-start = ((), (), s32[]{:S(2)}) async-start(), calls=%async_computation.49 | async-start | bytes 2359296 | tf_op jit(solution)/shard_map/all_gather | solution.py:150
  404.7 173.2 %reduce-scatter.27.cloned.1.call-start = ((), (), s32[]{:S(2)}) async-start(), calls=%async_computation.27 | async-start | bytes 1556480 | tf_op jit(solution)/shard_map/reduce_scatter | solution.py:264
  774.3 103.3 %reduce-scatter.45.cloned.1.call-start = ((), (), s32[]{:S(2)}) async-start(), calls=%async_computation.39 | async-start | bytes 1179648 | tf_op jit(solution)/shard_map/reduce_scatter | solution.py:334
  777.4 158.4 %reduce-scatter.43.cloned.1.call-start = ((), (), s32[]{:S(2)}) async-start(), calls=%async_computation.38 | async-start | bytes 1179648 | tf_op jit(solution)/shard_map/reduce_scatter | solution.py:334
  780.4 211.0 %reduce-scatter.37.cloned.1.call-start = ((), (), s32[]{:S(2)}) async-start(), calls=%async_computation.35 | async-start | bytes 36864 | tf_op jit(solution)/shard_map/reduce_scatter | solution.py:336
  781.5 265.5 %reduce-scatter.35.cloned.1.call-start = ((), (), s32[]{:S(2)}) async-start(), calls=%async_computation.34 | async-start | bytes 36864 | tf_op jit(solution)/shard_map/reduce_scatter | solution.py:336
  802.7 335.3 %reduce-scatter.53.cloned.1.call-start = ((), (), s32[]{:S(2)}) async-start(), calls=%async_computation.43 | async-start | bytes 4718592 | tf_op jit(solution)/shard_map/reduce_scatter | solution.py:335
  808.7 421.6 %reduce-scatter.51.cloned.1.call-start = ((), (), s32[]{:S(2)}) async-start(), calls=%async_computation.42 | async-start | bytes 4718592 | tf_op jit(solution)/shard_map/reduce_scatter | solution.py:335
  815.6 506.2 %reduce-scatter.49.cloned.1.call-start = ((), (), s32[]{:S(2)}) async-start(), calls=%async_computation.41 | async-start | bytes 4718592 | tf_op jit(solution)/shard_map/reduce_scatter | solution.py:333
  822.1 591.5 %reduce-scatter.47.cloned.1.call-start = ((), (), s32[]{:S(2)}) async-start(), calls=%async_computation.40 | async-start | bytes 4718592 | tf_op jit(solution)/shard_map/reduce_scatter | solution.py:333
  828.5 663.3 %reduce-scatter.41.cloned.1.call-start = ((), (), s32[]{:S(2)}) async-start(), calls=%async_computation.37 | async-start | bytes 3538944 | tf_op jit(solution)/shard_map/reduce_scatter | solution.py:332
  833.2 736.3 %reduce-scatter.39.cloned.1.call-start = ((), (), s32[]{:S(2)}) async-start(), calls=%async_computation.36 | async-start | bytes 3538944 | tf_op jit(solution)/shard_map/reduce_scatter | solution.py:332
  (99 other events, 2679.2 us)
Sparse Core Ops, SparseCore 0:
  57.3 45.6 all-gather.42
  114.4 24.9 reduce-scatter.18
  142.1 49.3 all-gather.44
  212.6 51.0 all-gather.46
  268.8 24.2 reduce-scatter.20
  295.9 46.0 all-gather.48
  374.0 26.1 reduce-scatter.22
  403.1 49.3 all-gather.50
  493.0 51.0 all-gather.52
  553.5 24.2 reduce-scatter.26
  580.3 26.1 reduce-scatter.24
  651.2 26.1 reduce-scatter.28
  707.7 26.0 reduce-scatter.30
  774.4 26.1 reduce-scatter.32
  804.6 63.9 reduce-scatter.44
  872.8 62.8 reduce-scatter.42
  938.9 52.4 reduce-scatter.36
  994.4 52.5 reduce-scatter.34
  1050.5 87.4 reduce-scatter.52
  1142.1 88.2 reduce-scatter.50
  1234.0 87.7 reduce-scatter.48
  1325.7 87.8 reduce-scatter.46
  1417.2 74.5 reduce-scatter.40
  1495.4 74.0 reduce-scatter.38
  (8 shorter events, 135.1 us)
where the time goes:
time: 1590 us; the launch traced here: 1580 us
  waiting for transfers between devices  1170 us (74%)
  blocking collectives  198 us (12%)
  matrix products  119 us (7%)
  other arithmetic  43.7 us (3%)
  local copies, waits for them, and re-layouts  33.7 us (2%)
  between operations  16.8 us (1%)
    reduce_scatter x2, waiting for transfers between devices, body(): lax.psum_scatter(grad_up_w, 'dp', scatter_dimension=0, tiled=True)  181 us
    reduce_scatter x2, waiting for transfers between devices, body(): lax.psum_scatter(grad_down_w, 'dp', scatter_dimension=1, tiled=True)  171 us
    reduce_scatter x2, waiting for transfers between devices, body(): lax.psum_scatter(grad_qkv_w, 'dp', scatter_dimension=0, tiled=True)  154 us
    reduce_scatter x2, waiting for transfers between devices, body(): lax.psum_scatter(grad_vec, 'dp', scatter_dimension=1, tiled=True)  108 us
    all_gather x2, waiting for transfers between devices, fetch(): lax.all_gather(down_weight[depth], 'dp', axis=1, tiled=True)  102 us
    all_gather x2, blocking collectives, fetch(): lax.all_gather(out_weight[depth], 'dp', axis=1, tiled=True)  59 us
    reduce_scatter x2, waiting for transfers between devices, body(): lax.psum_scatter(grad_out_w, 'dp', scatter_dimension=1, tiled=True)  58.1 us
    all_gather x2, blocking collectives, fetch(): lax.all_gather(up_bias[depth], 'dp', axis=0, tiled=True)  52.4 us
  transfers between devices with their start and end apart: 32, of which 30 were waited for; matrix products, arithmetic and copies ran while one was open for 5% of the time, Pallas kernels for 0%

commit v1 on v0

--- a/solution.py
+++ b/solution.py
@@ -4,6 +4,22 @@
 from jax.sharding import PartitionSpec as P
 
 HEAD_DIM = 64
+
+
+def gather_around(x, axis, dim):
+    ways, here, lap = (lax.axis_size(axis), lax.axis_index(axis), x.shape[dim])
+    shape = [n * ways if d == dim else n for d, n in enumerate(x.shape)]
+    full = lax.dynamic_update_slice_in_dim(jnp.zeros(shape, x.dtype), x, here * lap, axis=dim)
+    going_up = going_down = x
+    for far in range(1, ways // 2 + 1):
+        going_up = lax.ppermute(going_up, axis, [(d, (d + 1) % ways) for d in range(ways)])
+        full = lax.dynamic_update_slice_in_dim(full, going_up, (here - far) % ways * lap, axis=dim)
+        if 2 * far < ways:
+            going_down = lax.ppermute(going_down, axis, [(d, (d - 1) % ways) for d in range(ways)])
+            full = lax.dynamic_update_slice_in_dim(
+                full, going_down, (here + far) % ways * lap, axis=dim
+            )
+    return full
 
 
 def layer_norm(values, gain, shift):
@@ -145,7 +161,7 @@
     def fetch(depth):
         return (
             lax.all_gather(qkv_weight[depth], "dp", axis=0, tiled=True),
-            lax.all_gather(up_weight[depth], "dp", axis=0, tiled=True),
+            gather_around(up_weight[depth], "dp", 0),
             lax.all_gather(out_weight[depth], "dp", axis=1, tiled=True),
             lax.all_gather(down_weight[depth], "dp", axis=1, tiled=True),
             lax.all_gather(vectors[depth], "dp", axis=1, tiled=True),

time: 1590 us -> 1510 us (0.950)
  waiting for transfers between devices: 1170 us -> 1030 us
  starting transfers between devices: 2.11 us -> 31.2 us
    all_gather x2, waiting for transfers between devices: 102 us -> 27 us  [fetch(): lax.all_gather(down_weight[depth], 'dp', axis=1, tiled=True)]
    all_gather x2 -> x0, waiting for transfers between devices: 42.2 us -> none  [fetch(): lax.all_gather(up_weight[depth], 'dp', axis=0, tiled=True)]
    ppermute x0 -> x14, waiting for transfers between devices: none -> 38 us  [the longest x6 20.2 us: gather_around(): lax.ppermute(going_down, axis, [(d, (d - 1) % ways) for d in range(ways)])]
    all_gather x2, waiting for transfers between devices: 36.8 us -> 0.01 us  [forward_parts(): lax.all_gather(normed_mid, 'tensor', axis=0, tiled=True)]
    ppermute x0 -> x14, starting transfers between devices: none -> 29.2 us  [the longest x6 17.6 us: gather_around(): lax.ppermute(going_down, axis, [(d, (d - 1) % ways) for d in range(ways)])]
  transfers between devices with their start and end apart: 32 -> 44, of which waited for: 30 -> 34; matrix products, arithmetic and copies ran while one was open for 5% -> 6% of each run, Pallas kernels for 0% -> 0%
where the time goes in v1:
time: 1510 us; the launch traced here: 1500 us
  waiting for transfers between devices  1030 us (68%)
  blocking collectives  207 us (14%)
  matrix products  123 us (8%)
  other arithmetic  45.3 us (3%)
  local copies, waits for them, and re-layouts  44.6 us (3%)
  starting transfers between devices  31.2 us (2%)
  between operations  17.3 us (1%)
    reduce_scatter x2, waiting for transfers between devices, body(): lax.psum_scatter(grad_up_w, 'dp', scatter_dimension=0, tiled=True)  181 us
    reduce_scatter x2, waiting for transfers between devices, body(): lax.psum_scatter(grad_down_w, 'dp', scatter_dimension=1, tiled=True)  171 us
    reduce_scatter x2, waiting for transfers between devices, body(): lax.psum_scatter(grad_qkv_w, 'dp', scatter_dimension=0, tiled=True)  154 us
    reduce_scatter x2, waiting for transfers between devices, body(): lax.psum_scatter(grad_vec, 'dp', scatter_dimension=1, tiled=True)  108 us
    all_gather x2, blocking collectives, fetch(): lax.all_gather(up_bias[depth], 'dp', axis=0, tiled=True)  61.5 us
    all_gather x2, blocking collectives, fetch(): lax.all_gather(out_weight[depth], 'dp', axis=1, tiled=True)  58.9 us
    reduce_scatter x2, waiting for transfers between devices, body(): lax.psum_scatter(grad_out_w, 'dp', scatter_dimension=1, tiled=True)  58.7 us
    reduce_scatter x2, waiting for transfers between devices, forward_parts(): lax.psum_scatter(jnp.einsum('sie,ed->sid', mixed, out_w, preferred_elemen...  51.2 us
  transfers between devices with their start and end apart: 44, of which 34 were waited for; matrix products, arithmetic and copies ran while one was open for 6% of the time, Pallas kernels for 0%

profile of v1, /device:TPU:0, one launch (start us, length us, event | category | flops | bytes accessed | tf_op | source)
XLA Modules:
  0.0 1503.3 jit_solution(15372850661429971435)
XLA Ops:
  14.9 22.4 %all-gather = bf16[1,8,1024]{2,0,1:T(2,128)(2,1)S(1)} all-gather(bf16[1,8,128]{2,0,1:T(2,128)(2,1)S(1)} %get-tuple-element.224), channel_id=2, replica_groups=mesh['dp'=8,'tensor'=4] {'dp'}, dimensions={2}, use_global_device_ids=true | all-gather | bytes 18432 | tf_op jit(solution)/shard_map/all_gather | solution.py:167
  58.1 28.1 %all-gather.2 = bf16[1,256,1024]{2,1,0:T(8,128)(2,1)S(1)} all-gather(bf16[1,256,128]{2,1,0:T(8,128)(2,1)S(1)} %get-tuple-element.201), channel_id=4, replica_groups=mesh['dp'=8,'tensor'=4] {'dp'}, dimensions={2}, use_global_device_ids=true | all-gather | bytes 589824 | tf_op jit(solution)/shard_map/all_gather | solution.py:165
  114.3 25.0 %reduce-scatter.19.cloned.1.call-done = bf16[152,1,1024]{2,0,1:T(8,128)(2,1)} async-done(((bf16[608,1,1024]{2,0,1:T(8,128)(2,1)}), bf16[152,1,1024]{2,0,1:T(8,128)(2,1)}) %reduce-scatter.19.cloned.1.call-update) | async-done | bytes 311312 | tf_op jit(solution)/shard_map/reduce_scatter | solution.py:195
  150.1 30.7 %all-gather.3 = bf16[1,4096]{1,0:T(2,128)(2,1)S(1)} all-gather(bf16[1,512]{1,0:T(2,128)(2,1)S(1)} %get-tuple-element.227), channel_id=5, replica_groups=mesh['dp'=8,'tensor'=4] {'dp'}, dimensions={1}, use_global_device_ids=true | all-gather | bytes 9216 | tf_op jit(solution)/shard_map/all_gather | solution.py:168
  234.0 23.9 %reduce-scatter.21.cloned.1.call-done = bf16[152,1,1024]{2,0,1:T(8,128)(2,1)} async-done(((bf16[608,1,1024]{2,0,1:T(8,128)(2,1)}), bf16[152,1,1024]{2,0,1:T(8,128)(2,1)}) %reduce-scatter.21.cloned.1.call-update) | async-done | bytes 311312 | tf_op jit(solution)/shard_map/reduce_scatter | solution.py:233
  260.4 30.8 %all-gather.7 = bf16[1,256,1024]{2,1,0:T(8,128)(2,1)} all-gather(bf16[1,256,128]{2,1,0:T(8,128)(2,1)S(1)} %get-tuple-element.200), channel_id=9, replica_groups=mesh['dp'=8,'tensor'=4] {'dp'}, dimensions={2}, use_global_device_ids=true | all-gather | bytes 589824 | tf_op jit(solution)/shard_map/all_gather | solution.py:165
  306.6 18.8 %all-gather.27.cloned.1.call-done = bf16[608,1,1024]{2,0,1:T(8,128)(2,1)} async-done(((bf16[152,1,1024]{2,0,1:T(8,128)(2,1)}), bf16[608,1,1024]{2,0,1:T(8,128)(2,1)}) %all-gather.27.cloned.1.call-update) | async-done | bytes 1245200 | tf_op jit(solution)/shard_map/all_gather | solution.py:187
  338.5 26.2 %reduce-scatter.23.cloned.1.call-done = bf16[152,1,1024]{2,0,1:T(8,128)(2,1)} async-done(((bf16[608,1,1024]{2,0,1:T(8,128)(2,1)}), bf16[152,1,1024]{2,0,1:T(8,128)(2,1)}) %reduce-scatter.23.cloned.1.call-update) | async-done | bytes 311312 | tf_op jit(solution)/shard_map/reduce_scatter | solution.py:195
  375.0 30.8 %all-gather.8 = bf16[1,4096]{1,0:T(2,128)(2,1)S(1)} all-gather(bf16[1,512]{1,0:T(2,128)(2,1)S(1)} %get-tuple-element.226), channel_id=10, replica_groups=mesh['dp'=8,'tensor'=4] {'dp'}, dimensions={1}, use_global_device_ids=true | all-gather | bytes 9216 | tf_op jit(solution)/shard_map/all_gather | solution.py:168
  445.4 21.4 %all-gather.45.cloned.1.call-done = bf16[1,1024,1024]{2,1,0:T(8,128)(2,1)} async-done(((bf16[1,1024,128]{2,1,0:T(8,128)(2,1)}), bf16[1,1024,1024]{2,1,0:T(8,128)(2,1)}) %all-gather.45.cloned.1.call-update) | async-done | bytes 2097168 | tf_op jit(solution)/shard_map/all_gather | solution.py:166
  483.1 18.9 %reduce-scatter.27.cloned.1.call-done = bf16[152,1,1024]{2,0,1:T(8,128)(2,1)} async-done(((bf16[608,1,1024]{2,0,1:T(8,128)(2,1)}), bf16[152,1,1024]{2,0,1:T(8,128)(2,1)}) %reduce-scatter.27.cloned.1.call-update) | async-done | bytes 311312 | tf_op jit(solution)/shard_map/reduce_scatter | solution.py:280
  504.0 26.7 %reduce-scatter.25.cloned.1.call-done = bf16[152,1,1024]{2,0,1:T(8,128)(2,1)} async-done(((bf16[608,1,1024]{2,0,1:T(8,128)(2,1)}), bf16[152,1,1024]{2,0,1:T(8,128)(2,1)}) %reduce-scatter.25.cloned.1.call-update) | async-done | bytes 311312 | tf_op jit(solution)/shard_map/reduce_scatter | solution.py:233
  575.3 26.2 %reduce-scatter.29.cloned.1.call-done = bf16[152,1,1024]{2,0,1:T(8,128)(2,1)} async-done(((bf16[608,1,1024]{2,0,1:T(8,128)(2,1)}), bf16[152,1,1024]{2,0,1:T(8,128)(2,1)}) %reduce-scatter.29.cloned.1.call-update) | async-done | bytes 311312 | tf_op jit(solution)/shard_map/reduce_scatter | solution.py:310
  632.4 26.2 %reduce-scatter.31.cloned.1.call-done = bf16[152,1,1024]{2,0,1:T(8,128)(2,1)} async-done(((bf16[608,1,1024]{2,0,1:T(8,128)(2,1)}), bf16[152,1,1024]{2,0,1:T(8,128)(2,1)}) %reduce-scatter.31.cloned.1.call-update) | async-done | bytes 311312 | tf_op jit(solution)/shard_map/reduce_scatter | solution.py:280
  764.7 37.1 %all-reduce.2 = (f32[4096]{0:T(1024)S(1)}, f32[4096]{0:T(1024)S(1)}) all-reduce(f32[4096]{0:T(1024)S(1)} %dynamic_update_slice.112, f32[4096]{0:T(1024)S(1)} %dynamic_update_slice.111), channel_id=29, replica_groups=mesh['dp'=8,'tensor'=4] {'dp'}, use_global_device_ids=true, to_apply=%region_56.57.clone | all-reduce | flops 8192 | bytes 65536
  802.0 58.7 %reduce-scatter.43.cloned.1.call-done = f32[256,128]{1,0:T(8,128)} async-done(((f32[256,1024]{1,0:T(8,128)}), f32[256,128]{1,0:T(8,128)}) %reduce-scatter.43.cloned.1.call-update) | async-done | bytes 131088 | tf_op jit(solution)/shard_map/reduce_scatter | solution.py:350
  864.1 52.3 %reduce-scatter.37.cloned.1.call-done = f32[8,128]{1,0:T(8,128)} async-done(((f32[8,1024]{1,0:T(8,128)}), f32[8,128]{1,0:T(8,128)}) %reduce-scatter.37.cloned.1.call-update) | async-done | bytes 4112 | tf_op jit(solution)/shard_map/reduce_scatter | solution.py:352
  916.4 55.5 %reduce-scatter.35.cloned.1.call-done = f32[8,128]{1,0:T(8,128)} async-done(((f32[8,1024]{1,0:T(8,128)}), f32[8,128]{1,0:T(8,128)}) %reduce-scatter.35.cloned.1.call-update) | async-done | bytes 4112 | tf_op jit(solution)/shard_map/reduce_scatter | solution.py:352
  983.9 79.1 %reduce-scatter.53.cloned.1.call-done = f32[1024,128]{1,0:T(8,128)} async-done(((f32[1024,1024]{1,0:T(8,128)}), f32[1024,128]{1,0:T(8,128)}) %reduce-scatter.53.cloned.1.call-update) | async-done | bytes 524304 | tf_op jit(solution)/shard_map/reduce_scatter | solution.py:351
  1063.0 92.2 %reduce-scatter.51.cloned.1.call-done = f32[1024,128]{1,0:T(8,128)} async-done(((f32[1024,1024]{1,0:T(8,128)}), f32[1024,128]{1,0:T(8,128)}) %reduce-scatter.51.cloned.1.call-update) | async-done | bytes 524304 | tf_op jit(solution)/shard_map/reduce_scatter | solution.py:351
  1157.5 88.9 %reduce-scatter.49.cloned.1.call-done = f32[128,1024]{1,0:T(8,128)} async-done(((f32[1024,1024]{1,0:T(8,128)}), f32[128,1024]{1,0:T(8,128)}) %reduce-scatter.49.cloned.1.call-update) | async-done | bytes 524304 | tf_op jit(solution)/shard_map/reduce_scatter | solution.py:349
  1246.4 91.8 %reduce-scatter.47.cloned.1.call-done = f32[128,1024]{1,0:T(8,128)} async-done(((f32[1024,1024]{1,0:T(8,128)}), f32[128,1024]{1,0:T(8,128)}) %reduce-scatter.47.cloned.1.call-update) | async-done | bytes 524304 | tf_op jit(solution)/shard_map/reduce_scatter | solution.py:349
  1340.4 76.0 %reduce-scatter.41.cloned.1.call-done = f32[128,3,256]{2,0,1:T(8,128)} async-done(((f32[1024,3,256]{2,0,1:T(8,128)}), f32[128,3,256]{2,0,1:T(8,128)}) %reduce-scatter.41.cloned.1.call-update) | async-done | bytes 393232 | tf_op jit(solution)/shard_map/reduce_scatter | solution.py:348
  1416.4 77.6 %reduce-scatter.39.cloned.1.call-done = f32[128,3,256]{2,0,1:T(8,128)} async-done(((f32[1024,3,256]{2,0,1:T(8,128)}), f32[128,3,256]{2,0,1:T(8,128)}) %reduce-scatter.39.cloned.1.call-update) | async-done | bytes 393232 | tf_op jit(solution)/shard_map/reduce_scatter | solution.py:348
  (433 shorter events, 420.6 us)
Async XLA Ops:
  7.2 79.0 %all-gather.23.cloned.1.call-start = ((), (), s32[]{:S(2)}) async-start(), calls=%async_computation.18 | async-start | bytes 1556480 | tf_op jit(solution)/shard_map/all_gather | solution.py:187
  41.2 98.1 %reduce-scatter.19.cloned.1.call-start = ((), (), s32[]{:S(2)}) async-start(), calls=%async_computation.19 | async-start | bytes 1556480 | tf_op jit(solution)/shard_map/reduce_scatter | solution.py:195
  114.3 103.6 %all-gather.25.cloned.1.call-start = ((), (), s32[]{:S(2)}) async-start(), calls=%async_computation.20 | async-start | bytes 1556480 | tf_op jit(solution)/shard_map/all_gather | solution.py:209
  143.6 84.7 %all-gather.41.cloned.1.call-start = ((), (), s32[]{:S(2)}) async-start(), calls=%async_computation.45 | async-start | bytes 2359296 | tf_op jit(solution)/shard_map/all_gather | solution.py:166
  144.5 113.5 %reduce-scatter.21.cloned.1.call-start = ((), (), s32[]{:S(2)}) async-start(), calls=%async_computation.21 | async-start | bytes 1556480 | tf_op jit(solution)/shard_map/reduce_scatter | solution.py:233
  233.2 73.4 %all-gather.43.cloned.1.call-start = ((), (), s32[]{:S(2)}) async-start(), calls=%async_computation.46 | async-start | bytes 1769472 | tf_op jit(solution)/shard_map/all_gather | solution.py:163
  234.0 91.4 %all-gather.27.cloned.1.call-start = ((), (), s32[]{:S(2)}) async-start(), calls=%async_computation.22 | async-start | bytes 1556480 | tf_op jit(solution)/shard_map/all_gather | solution.py:187
  260.4 104.3 %reduce-scatter.23.cloned.1.call-start = ((), (), s32[]{:S(2)}) async-start(), calls=%async_computation.23 | async-start | bytes 1556480 | tf_op jit(solution)/shard_map/reduce_scatter | solution.py:195
  338.4 102.2 %all-gather.29.cloned.1.call-start = ((), (), s32[]{:S(2)}) async-start(), calls=%async_computation.24 | async-start | bytes 1556480 | tf_op jit(solution)/shard_map/all_gather | solution.py:209
  367.0 78.4 %all-gather.31.cloned.1.call-start = ((), (), s32[]{:S(2)}) async-start(), calls=%async_computation.26 | async-start | bytes 1556480 | tf_op jit(solution)/shard_map/all_gather | solution.py:267
  369.6 97.3 %all-gather.45.cloned.1.call-start = ((), (), s32[]{:S(2)}) async-start(), calls=%async_computation.47 | async-start | bytes 2359296 | tf_op jit(solution)/shard_map/all_gather | solution.py:166
  370.2 131.8 %reduce-scatter.27.cloned.1.call-start = ((), (), s32[]{:S(2)}) async-start(), calls=%async_computation.27 | async-start | bytes 1556480 | tf_op jit(solution)/shard_map/reduce_scatter | solution.py:280
  483.1 70.0 %all-gather.33.cloned.1.call-start = ((), (), s32[]{:S(2)}) async-start(), calls=%async_computation.28 | async-start | bytes 1556480 | tf_op jit(solution)/shard_map/all_gather | solution.py:293
  535.1 66.4 %reduce-scatter.29.cloned.1.call-start = ((), (), s32[]{:S(2)}) async-start(), calls=%async_computation.29 | async-start | bytes 1556480 | tf_op jit(solution)/shard_map/reduce_scatter | solution.py:310
  699.0 103.0 %reduce-scatter.45.cloned.1.call-start = ((), (), s32[]{:S(2)}) async-start(), calls=%async_computation.39 | async-start | bytes 1179648 | tf_op jit(solution)/shard_map/reduce_scatter | solution.py:350
  702.0 158.7 %reduce-scatter.43.cloned.1.call-start = ((), (), s32[]{:S(2)}) async-start(), calls=%async_computation.38 | async-start | bytes 1179648 | tf_op jit(solution)/shard_map/reduce_scatter | solution.py:350
  705.1 211.3 %reduce-scatter.37.cloned.1.call-start = ((), (), s32[]{:S(2)}) async-start(), calls=%async_computation.35 | async-start | bytes 36864 | tf_op jit(solution)/shard_map/reduce_scatter | solution.py:352
  707.1 264.9 %reduce-scatter.35.cloned.1.call-start = ((), (), s32[]{:S(2)}) async-start(), calls=%async_computation.34 | async-start | bytes 36864 | tf_op jit(solution)/shard_map/reduce_scatter | solution.py:352
  727.4 335.6 %reduce-scatter.53.cloned.1.call-start = ((), (), s32[]{:S(2)}) async-start(), calls=%async_computation.43 | async-start | bytes 4718592 | tf_op jit(solution)/shard_map/reduce_scatter | solution.py:351
  733.4 421.8 %reduce-scatter.51.cloned.1.call-start = ((), (), s32[]{:S(2)}) async-start(), calls=%async_computation.42 | async-start | bytes 4718592 | tf_op jit(solution)/shard_map/reduce_scatter | solution.py:351
  740.1 506.3 %reduce-scatter.49.cloned.1.call-start = ((), (), s32[]{:S(2)}) async-start(), calls=%async_computation.41 | async-start | bytes 4718592 | tf_op jit(solution)/shard_map/reduce_scatter | solution.py:349
  745.7 592.5 %reduce-scatter.47.cloned.1.call-start = ((), (), s32[]{:S(2)}) async-start(), calls=%async_computation.40 | async-start | bytes 4718592 | tf_op jit(solution)/shard_map/reduce_scatter | solution.py:349
  751.2 665.2 %reduce-scatter.41.cloned.1.call-start = ((), (), s32[]{:S(2)}) async-start(), calls=%async_computation.37 | async-start | bytes 3538944 | tf_op jit(solution)/shard_map/reduce_scatter | solution.py:348
  756.7 737.3 %reduce-scatter.39.cloned.1.call-start = ((), (), s32[]{:S(2)}) async-start(), calls=%async_computation.36 | async-start | bytes 3538944 | tf_op jit(solution)/shard_map/reduce_scatter | solution.py:348
  (103 other events, 2509.7 us)
Sparse Core Ops, SparseCore 0:
  57.3 45.5 all-gather.38
  114.4 24.8 reduce-scatter.18
  143.7 17.8 all-gather.24
  164.3 63.9 all-gather.40
  233.3 24.5 reduce-scatter.20
  260.7 45.8 all-gather.42
  338.6 26.1 reduce-scatter.22
  407.2 59.6 all-gather.44
  477.7 24.2 reduce-scatter.26
  504.5 26.1 reduce-scatter.24
  575.4 26.1 reduce-scatter.28
  632.4 26.1 reduce-scatter.30
  663.4 17.8 all-gather.36
  699.1 26.1 reduce-scatter.32
  729.3 63.9 reduce-scatter.44
  797.7 62.9 reduce-scatter.42
  863.8 52.5 reduce-scatter.36
  919.4 52.5 reduce-scatter.34
  975.6 87.4 reduce-scatter.52
  1066.9 88.2 reduce-scatter.50
  1158.7 87.6 reduce-scatter.48
  1250.4 87.6 reduce-scatter.46
  1341.8 74.6 reduce-scatter.40
  1419.9 74.1 reduce-scatter.38
  (6 shorter events, 102.6 us)
